TPU v7x, 256 devices: a whole 4x4x8 slice. The times are simulated.
256 devices in a mesh: clip: 32 (over z_hi, x, y), tm: 8 (over z_lo, core).
Axes of the slice: x: 4, y: 4, z: 8 (z_hi: 2, z_lo: 4; z = z_hi * 4 + z_lo), core: 2. Of those that a mesh axis runs over, the one named last changes fastest.
Arguments:
- audio_feats: bfloat16 [128, 2048, 256], P('clip', 'tm'), may hold values from -6 to 6
- lip_feats: bfloat16 [128, 2048, 256], P('clip', 'tm'), may hold values from -6 to 6
- lengths: int32 [128], P('clip'), may hold values from 1024 to 2048
- labels: int32 [128], P('clip'), may hold values from -15 to 15
- w_audio_conv: bfloat16 [3, 256, 512], replicated, may hold values from -0.21875 to 0.21875
- w_audio_proj: bfloat16 [512, 512], replicated, may hold values from -0.25 to 0.25
- w_lip_conv: bfloat16 [3, 256, 512], replicated, may hold values from -0.21875 to 0.21875
- w_lip_proj: bfloat16 [512, 512], replicated, may hold values from -0.25 to 0.25
Outputs:
- loss: float32 [], replicated
- grad_audio_conv: float32 [3, 256, 512], replicated
- grad_audio_proj: float32 [512, 512], replicated
- grad_lip_conv: float32 [3, 256, 512], replicated
- grad_lip_proj: float32 [512, 512], replicated
All inputs are finite; a program needn't handle non-finite values.
Results may differ from a plain program's by a relative error of at most 0.0075.
Values may be sent and summed in bfloat16 or wider, within the bound.
A program may use at most 64 MiB of HBM per device.

v0:
```python
import jax
import jax.numpy as jnp
from jax import lax
from jax.sharding import PartitionSpec as P

SPAN = 15
logit_sharpening_divisor = 10.0
loss_scale = 1024.0
epsilon = 1e-06


def padded_2(cells, sides, width):
    for axis, dim in sides:
        count = lax.axis_size(axis)
        ends = count - 1
        head = lax.slice_in_dim(cells, 0, width, axis=dim)
        tail = lax.slice_in_dim(cells, cells.shape[dim] - width, cells.shape[dim], axis=dim)
        cells = jnp.concatenate(
            [
                lax.ppermute(tail, axis, [(i, (i + 1) % count) for i in range(ends)]),
                cells,
                lax.ppermute(head, axis, [((i + 1) % count, i) for i in range(ends)]),
            ],
            axis=dim,
        )
    return cells


def from_behind(value, axis, steps):
    count = lax.axis_size(axis)
    initial, last = (max(0, -steps), min(count, count - steps))
    return lax.ppermute(value, axis, [(source, source + steps) for source in range(initial, last)])


def silu_slope(values):
    sigma = jax.nn.sigmoid(values)
    return sigma * (1.0 + values * (1.0 - sigma))


def encoder(padded, w_conv, w_proj):
    clip_num, frame_pad, chan_num = padded.shape
    frame_num = frame_pad - 2
    columns = jnp.concatenate(
        [padded[:, 0:frame_num], padded[:, 1 : frame_num + 1], padded[:, 2 : frame_num + 2]], axis=2
    )
    before = jnp.einsum(
        "cfk,ke->cfe",
        columns,
        w_conv.reshape(3 * chan_num, w_conv.shape[2]),
        preferred_element_type=jnp.float32,
    )
    hidden = jax.nn.silu(before).astype(jnp.bfloat16)
    embedded = jnp.einsum("cfe,eg->cfg", hidden, w_proj, preferred_element_type=jnp.float32).astype(
        jnp.bfloat16
    )
    return (columns, before, hidden, embedded)


def inverse_norm(embedded):
    values = embedded.astype(jnp.float32)
    return lax.rsqrt(jnp.sum(values * values, axis=-1) + epsilon)


def spread_band(band, wide_len):
    clip_num, row_num, band_len = band.shape
    full_band = jnp.pad(band, ((0, 0), (0, 0), (0, wide_len + 1 - band_len)))
    flat_band = full_band.reshape(clip_num, row_num * (wide_len + 1))[:, : row_num * wide_len]
    return flat_band.reshape(clip_num, row_num, wide_len)


def narrow_band(matrix, band_len):
    clip_num, row_num, wide_len = matrix.shape
    flat_mat = jnp.pad(matrix.reshape(clip_num, row_num * wide_len), ((0, 0), (0, row_num)))
    return flat_mat.reshape(clip_num, row_num, wide_len + 1)[:, :, :band_len]


def flatten_rows(values):
    return values.reshape(values.shape[0] * values.shape[1], values.shape[2])


def proj_grad(hidden, grad_emb):
    return jnp.einsum("re,rf->ef", hidden, grad_emb, preferred_element_type=jnp.float32)


def conv_grad(columns, before, grad_emb, w_proj, w_conv):
    grad_hidden = jnp.einsum("rf,ef->re", grad_emb, w_proj, preferred_element_type=jnp.float32)
    grad_before = (grad_hidden * silu_slope(before)).astype(jnp.bfloat16)
    grad_conv = jnp.einsum("rk,re->ke", columns, grad_before, preferred_element_type=jnp.float32)
    return grad_conv.reshape(w_conv.shape)


def shards(
    audio_feats, lip_feats, lengths, labels, w_audio_conv, w_audio_proj, w_lip_conv, w_lip_proj
):
    clip_num, frame_num, chan_num = audio_feats.shape
    width = w_audio_proj.shape[1]
    offsets = 2 * SPAN + 1
    wide_len = frame_num + 2 * SPAN
    first_frame = lax.axis_index("tm") * frame_num
    stacked = jnp.stack([audio_feats, lip_feats])
    padded = padded_2(stacked, (("tm", 2),), 1)
    cols_a, pre_a, hid_a, emb_a = encoder(padded[0], w_audio_conv, w_audio_proj)
    cols_v, pre_v, hid_v, emb_v = encoder(padded[1], w_lip_conv, w_lip_proj)
    window = padded_2(emb_a, (("tm", 1),), SPAN)
    cols_a, pre_a, hid_a = (flatten_rows(cols_a), flatten_rows(pre_a), flatten_rows(hid_a))
    cols_v, pre_v, hid_v = (flatten_rows(cols_v), flatten_rows(pre_v), flatten_rows(hid_v))
    count = lax.psum(jnp.sum((lengths - jnp.abs(labels)).astype(jnp.float32)), "clip")
    matrix = jnp.einsum("cfe,cwe->cfw", emb_v, window, preferred_element_type=jnp.float32)
    lagged_inner_terms = narrow_band(matrix, offsets)
    inv_win = inverse_norm(window)
    reciprocal_visual_length = inverse_norm(emb_v)
    reciprocal_lag_strip = jnp.stack(
        [inv_win[:, offset : offset + frame_num] for offset in range(offsets)], axis=2
    )
    frame_ids = first_frame + jnp.arange(frame_num, dtype=jnp.int32)
    shifts = jnp.arange(offsets, dtype=jnp.int32) - SPAN
    positions = frame_ids[:, None] + shifts[None, :]
    inside = frame_ids[None, :] < lengths[:, None]
    valid = inside[:, :, None] & (positions[None] >= 0) & (positions[None] < lengths[:, None, None])
    target_pos = frame_ids[None, :] + labels[:, None]
    counted = inside & (target_pos >= 0) & (target_pos < lengths[:, None])
    correct_lag_position = (shifts[None, :] == labels[:, None]).astype(jnp.float32)
    lag_similarity_logits = (
        logit_sharpening_divisor
        * lagged_inner_terms
        * reciprocal_visual_length[:, :, None]
        * reciprocal_lag_strip
    )
    exponentiated_logits = jnp.where(valid, jnp.exp(lag_similarity_logits), 0.0)
    partition_sums = jnp.where(inside, jnp.sum(exponentiated_logits, axis=2), 1.0)
    picked = jnp.sum(lag_similarity_logits * correct_lag_position[:, None, :], axis=2)
    loss_local = jnp.sum(jnp.where(counted, jnp.log(partition_sums) - picked, 0.0))
    normalized_probabilities = jnp.where(counted, loss_scale / count, 0.0)
    logit_derivative = (
        logit_sharpening_divisor
        * normalized_probabilities[:, :, None]
        * (exponentiated_logits / partition_sums[:, :, None] - correct_lag_position[:, None, :])
    )
    grad_dots = (
        logit_derivative * reciprocal_visual_length[:, :, None] * reciprocal_lag_strip
    ).astype(jnp.bfloat16)
    grad_inv_v = jnp.sum(logit_derivative * lagged_inner_terms * reciprocal_lag_strip, axis=2)
    grad_inv_win = jnp.sum(
        spread_band(
            logit_derivative * lagged_inner_terms * reciprocal_visual_length[:, :, None], wide_len
        ),
        axis=1,
    )
    band_full = spread_band(grad_dots, wide_len)
    lip_sum = jnp.einsum("cfw,cwe->cfe", band_full, window, preferred_element_type=jnp.float32)
    lip_vals = emb_v.astype(jnp.float32)
    grad_lip = (
        lip_sum
        - (
            reciprocal_visual_length
            * reciprocal_visual_length
            * reciprocal_visual_length
            * grad_inv_v
        )[:, :, None]
        * lip_vals
    ).astype(jnp.bfloat16)
    win_sum = jnp.einsum("cfw,cfe->cwe", band_full, emb_v, preferred_element_type=jnp.float32)
    win_sum = win_sum - (inv_win * inv_win * inv_win * grad_inv_win)[:, :, None] * window.astype(
        jnp.float32
    )
    own_grad = win_sum[:, SPAN : SPAN + frame_num]
    from_after = from_behind(win_sum[:, :SPAN], "tm", -1)
    from_before = from_behind(win_sum[:, frame_num + SPAN :], "tm", 1)
    own_grad = own_grad.at[:, frame_num - SPAN :].add(from_after)
    own_grad = own_grad.at[:, :SPAN].add(from_before)
    grad_audio = own_grad.astype(jnp.bfloat16).reshape(clip_num * frame_num, width)
    grad_lip = grad_lip.reshape(clip_num * frame_num, width)
    grad_ap = proj_grad(hid_a, grad_audio)
    grad_vp = proj_grad(hid_v, grad_lip)
    grad_ac = conv_grad(cols_a, pre_a, grad_audio, w_audio_proj, w_audio_conv)
    grad_vc = conv_grad(cols_v, pre_v, grad_lip, w_lip_proj, w_lip_conv)
    grad_ac, grad_vc, grad_ap, grad_vp, loss_sum = lax.psum(
        (grad_ac, grad_vc, grad_ap, grad_vp, loss_local), ("clip", "tm")
    )
    return (loss_sum / count, grad_ac, grad_ap, grad_vc, grad_vp)


def solution(mesh):
    placed = (
        P("clip", "tm", None),
        P("clip", "tm", None),
        P("clip"),
        P("clip"),
        P(),
        P(),
        P(),
        P(),
    )
    return jax.shard_map(
        shards, mesh=mesh, in_specs=placed, out_specs=(P(), P(), P(), P(), P()), check_vma=False
    )
```

profile of v0, /device:TPU:2, one launch (start us, length us, event | category | flops | bytes accessed | tf_op | source)
XLA Modules:
  0.0 491.8 jit_solution(7356766110926714444)
XLA Ops:
  8.1 1.7 collective-permute-start
  15.8 104.9 %psum.43 = f32[]{:T(128)} all-reduce(f32[]{:T(128)} %convert_reduce_fusion), channel_id=1, replica_groups=mesh['clip'=32,'tm'=8] {'clip'}, use_global_device_ids=true, to_apply=%region_7.8 | all-reduce | flops 1 | bytes 8 | tf_op jit(solution)/shard_map/psum | solution.py:107
  124.7 1.8 fusion.2
  130.2 1.9 collective-permute-start.2
  134.6 1.7 copy.1171
  136.3 2.6 copy.1167
  142.9 2.3 fusion.28
  145.1 2.5 reshape.357
  149.2 2.6 reshape.358
  151.9 1.6 fusion.23
  153.5 2.8 multiply_reduce_fusion
  157.9 1.7 reshape.361
  159.6 2.7 fusion.4
  162.3 1.7 convolution_bitcast_fusion
  164.1 2.2 fusion.20
  168.9 3.1 reshape.363
  172.1 2.4 fusion.1
  174.5 6.2 %collective-permute-start.5 = (f32[4,15,512]{2,1,0:T(8,128)S(1)}, f32[4,15,512]{2,1,0:T(8,128)S(1)}, u32[]{:S(2)}, u32[]{:S(2)}) collective-permute-start(f32[4,15,512]{2,1,0:T(8,128)S(1)} %get-tuple-element.37), channel_id=1, source_target_pairs={{0,1},{1,2},{2,3},{3,4},{4,5},{5,6},{6,7},{8,9},{9,10},{10,11},{11... | collective-permute-start | bytes 368648 | tf_op jit(solution)/shard_map/ppermute | solution.py:32
  182.0 2.2 fusion.36
  187.7 1.7 convolution_bitcast_fusion.1
  190.9 2.1 fusion.35
  194.3 90.7 %psum.42 = f32[]{:T(128)} all-reduce(f32[]{:T(128)} %select_reduce_fusion), channel_id=1, replica_groups=mesh['clip'=32,'tm'=8] {'clip','tm'}, use_global_device_ids=true, to_apply=%region_5.6 | all-reduce | flops 1 | bytes 8 | tf_op jit(solution)/shard_map/psum | solution.py:177
  286.3 190.9 %all-reduce.6.cloned.1.call-done = (f32[3,256,512]{2,1,0:T(8,128)}, f32[512,512]{1,0:T(8,128)}, f32[3,256,512]{2,1,0:T(8,128)}, f32[512,512]{1,0:T(8,128)}) async-done(((f32[3,256,512]{2,1,0:T(8,128)}, f32[512,512]{1,0:T(8,128)}, f32[3,256,512]{2,1,0:T(8,128)}, f32[512,512]{1,0:T(8,128)}), (f32[3,256,512]{2,1,0:T(8,128)}, f32[512,512]{1,0:T(8,128)}, f32[3,256,512]{2,1,0:T(8,128)}, ...) | async-done | bytes 5242896 | tf_op jit(solution)/shard_map/psum | solution.py:177
  477.3 2.8 copy.1216
  (148 shorter events, 37.4 us)
Async XLA Ops:
  7.2 116.5 %copy-start = (bf16[3,256,512]{2,1,0:T(8,128)(2,1)S(1)}, bf16[3,256,512]{2,1,0:T(8,128)(2,1)}, u32[]{:S(2)}) copy-start(bf16[3,256,512]{2,1,0:T(8,128)(2,1)} %param.18) | copy-start | bytes 2359300
  7.2 470.1 %all-reduce.6.cloned.1.call-start = ((), (), s32[]{:S(2)}) async-start(), calls=%async_computation | async-start | bytes 10485760 | tf_op jit(solution)/shard_map/psum | solution.py:177
  8.1 113.3 %collective-permute-start = (bf16[2,4,1,256]{3,2,1,0:T(2,128)(2,1)S(1)}, bf16[2,4,1,256]{3,2,1,0:T(2,128)(2,1)S(1)}, u32[]{:S(2)}, u32[]{:S(2)}) collective-permute-start(bf16[2,4,1,256]{3,2,1,0:T(2,128)(2,1)S(1)} %get-tuple-element.45), channel_id=1, source_target_pairs={{0,1},{1,2},{2,3},{3,4},{4,5},{5,6},{6,7},{8,9},{9,10},{10,11},{11... | collective-permute-start | bytes 12296 | tf_op jit(solution)/shard_map/ppermute | solution.py:20
  9.8 111.5 %collective-permute-start.1 = (bf16[2,4,1,256]{3,2,1,0:T(2,128)(2,1)S(1)}, bf16[2,4,1,256]{3,2,1,0:T(2,128)(2,1)S(1)}, u32[]{:S(2)}, u32[]{:S(2)}) collective-permute-start(bf16[2,4,1,256]{3,2,1,0:T(2,128)(2,1)S(1)} %get-tuple-element.46), channel_id=1, source_target_pairs={{1,0},{2,1},{3,2},{4,3},{5,4},{6,5},{7,6},{9,8},{10,9},{11,10},{12... | collective-permute-start | bytes 12296 | tf_op jit(solution)/shard_map/ppermute | solution.py:22
  129.5 9.4 %copy-start.4 = (bf16[4,256,512]{2,1,0:T(8,128)(2,1)}, bf16[4,256,512]{2,1,0:T(8,128)(2,1)S(1)}, u32[]{:S(2)}) copy-start(bf16[4,256,512]{2,1,0:T(8,128)(2,1)S(1)} %convolution_convert_fusion) | copy-start | bytes 3145732
  130.2 8.7 %collective-permute-start.2 = (bf16[4,15,512]{2,1,0:T(8,128)(2,1)}, bf16[4,15,512]{2,1,0:T(8,128)(2,1)}, u32[]{:S(2)}, u32[]{:S(2)}) collective-permute-start(bf16[4,15,512]{2,1,0:T(8,128)(2,1)} %get-tuple-element.43), channel_id=1, source_target_pairs={{0,1},{1,2},{2,3},{3,4},{4,5},{5,6},{6,7},{8,9},{9,10},{10,11},{11... | collective-permute-start | bytes 184328 | tf_op jit(solution)/shard_map/ppermute | solution.py:20
  132.1 6.8 %collective-permute-start.3 = (bf16[4,15,512]{2,1,0:T(8,128)(2,1)}, bf16[4,15,512]{2,1,0:T(8,128)(2,1)}, u32[]{:S(2)}, u32[]{:S(2)}) collective-permute-start(bf16[4,15,512]{2,1,0:T(8,128)(2,1)} %get-tuple-element.44), channel_id=1, source_target_pairs={{1,0},{2,1},{3,2},{4,3},{5,4},{6,5},{7,6},{9,8},{10,9},{11,10},{12... | collective-permute-start | bytes 184328 | tf_op jit(solution)/shard_map/ppermute | solution.py:22
  147.7 4.2 copy-start.9
  147.7 4.2 copy-start.11
  147.7 4.2 copy-start.15
  147.7 4.2 copy-start.17
  149.2 4.3 copy-start.19
  149.2 4.3 copy-start.10
  149.2 4.3 copy-start.18
  151.9 4.5 copy-start.14
  159.6 2.7 copy-start.8
  159.6 2.7 copy-start.30
  168.9 3.2 copy-start.5
  172.1 9.9 %copy-start.2 = (bf16[768,1024]{1,0:T(8,128)(2,1)S(1)}, bf16[768,1024]{1,0:T(8,128)(2,1)}, u32[]{:S(2)}) copy-start(bf16[768,1024]{1,0:T(8,128)(2,1)} %copy.1171) | copy-start | bytes 4718596
  172.1 9.9 %copy-start.26 = (bf16[1024,512,1]{1,0,2:T(8,128)(2,1)S(1)}, bf16[1024,512,1]{1,0,2:T(8,128)(2,1)}, u32[]{:S(2)}) copy-start(bf16[1024,512,1]{1,0,2:T(8,128)(2,1)} %fusion.20) | copy-start | bytes 3145732
  174.5 11.2 %collective-permute-start.5 = (f32[4,15,512]{2,1,0:T(8,128)S(1)}, f32[4,15,512]{2,1,0:T(8,128)S(1)}, u32[]{:S(2)}, u32[]{:S(2)}) collective-permute-start(f32[4,15,512]{2,1,0:T(8,128)S(1)} %get-tuple-element.37), channel_id=1, source_target_pairs={{0,1},{1,2},{2,3},{3,4},{4,5},{5,6},{6,7},{8,9},{9,10},{10,11},{11... | collective-permute-start | bytes 368648 | tf_op jit(solution)/shard_map/ppermute | solution.py:32
  180.7 4.5 collective-permute-start.4
  477.3 2.8 copy-start.7
  477.3 3.8 copy-start.3
  (14 other events, 19.5 us)
Sparse Core Ops, SparseCore 0:
  193.1 284.1 all-reduce.5
where the time goes:
time: 493 us; the launch traced here: 492 us
  blocking collectives  196 us (40%)
  waiting for transfers between devices  192 us (39%)
  local copies, waits for them, and re-layouts  34.6 us (7%)
  matrix products  22.9 us (5%)
  between operations  17.7 us (4%)
  other arithmetic  15.7 us (3%)
  starting transfers between devices  13.7 us (3%)
    psum x1, waiting for transfers between devices, shards(): lax.psum((grad_ac, grad_vc, grad_ap, grad_vp, loss_local), ('clip', 'tm'))  191 us
    psum x1, blocking collectives, shards(): lax.psum(jnp.sum((lengths - jnp.abs(labels)).astype(jnp.float32)), 'clip')  105 us
    psum x1, blocking collectives, shards(): lax.psum((grad_ac, grad_vc, grad_ap, grad_vp, loss_local), ('clip', 'tm'))  90.7 us
    unnamed x96, local copies, waits for them, and re-layouts  12 us
  transfers between devices with their start and end apart: 7, of which 2 were waited for; matrix products, arithmetic and copies ran while one was open for 3% of the time, Pallas kernels for 0%

commit v1 on v0

--- a/solution.py
+++ b/solution.py
@@ -175,7 +175,7 @@
     grad_ac = conv_grad(cols_a, pre_a, grad_audio, w_audio_proj, w_audio_conv)
     grad_vc = conv_grad(cols_v, pre_v, grad_lip, w_lip_proj, w_lip_conv)
     grad_ac, grad_vc, grad_ap, grad_vp, loss_sum = lax.psum(
-        (grad_ac, grad_vc, grad_ap, grad_vp, loss_local), ("clip", "tm")
+        lax.psum((grad_ac, grad_vc, grad_ap, grad_vp, loss_local), "clip"), "tm"
     )
     return (loss_sum / count, grad_ac, grad_ap, grad_vc, grad_vp)
 

time: 493 us -> 840 us (1.70)
  waiting for transfers between devices: 192 us -> 506 us
  blocking collectives: 196 us -> 234 us
    psum x1 -> x2, waiting for transfers between devices: 191 us -> 505 us  [the longest x1 490 us: shards(): lax.psum((grad_ac, grad_vc, grad_ap, grad_vp, loss_local), 'clip')]
    psum x1 -> x2, blocking collectives: 90.7 us -> 129 us  [the longest x1 114 us: shards(): lax.psum((grad_ac, grad_vc, grad_ap, grad_vp, loss_local), 'clip')]
  transfers between devices with their start and end apart: 7 -> 8, of which waited for: 2 -> 3; matrix products, arithmetic and copies ran while one was open for 3% -> 2% of each run, Pallas kernels for 0% -> 0%
where the time goes in v1:
time: 840 us; the launch traced here: 838 us
  waiting for transfers between devices  506 us (60%)
  blocking collectives  234 us (28%)
  local copies, waits for them, and re-layouts  30.6 us (4%)
  matrix products  22 us (3%)
  between operations  17.9 us (2%)
  other arithmetic  14.6 us (2%)
  starting transfers between devices  13.8 us (2%)
    psum x1, waiting for transfers between devices, shards(): lax.psum((grad_ac, grad_vc, grad_ap, grad_vp, loss_local), 'clip')  490 us
    psum x1, blocking collectives, shards(): lax.psum((grad_ac, grad_vc, grad_ap, grad_vp, loss_local), 'clip')  114 us
    psum x1, blocking collectives, shards(): lax.psum(jnp.sum((lengths - jnp.abs(labels)).astype(jnp.float32)), 'clip')  105 us
  transfers between devices with their start and end apart: 8, of which 3 were waited for; matrix products, arithmetic and copies ran while one was open for 2% of the time, Pallas kernels for 0%

profile of v1, /device:TPU:2, one launch (start us, length us, event | category | flops | bytes accessed | tf_op | source)
XLA Modules:
  0.0 838.1 jit_solution(9309386993413096230)
XLA Ops:
  8.1 1.7 collective-permute-start
  16.5 104.9 %psum.79 = f32[]{:T(128)} all-reduce(f32[]{:T(128)} %convert_reduce_fusion), channel_id=1, replica_groups=mesh['clip'=32,'tm'=8] {'clip'}, use_global_device_ids=true, to_apply=%region_8.9 | all-reduce | flops 1 | bytes 8 | tf_op jit(solution)/shard_map/psum | solution.py:107
  125.4 1.8 fusion.2
  133.5 1.6 copy.1171
  135.1 2.7 copy.1167
  141.0 1.9 fusion.28
  142.9 1.6 reshape.357
  144.8 1.5 reshape.358
  146.9 2.2 multiply_reduce_fusion
  150.7 1.7 reshape.361
  152.4 2.3 fusion.4
  154.8 1.8 convolution_bitcast_fusion
  156.5 2.2 fusion.20
  161.4 3.1 reshape.363
  166.0 2.1 fusion.1
  168.1 6.8 collective-permute-start.5
  176.2 2.2 fusion.36
  181.9 1.8 convolution_bitcast_fusion.1
  185.1 2.1 fusion.35
  187.3 489.6 %all-reduce.8.cloned.1.call-done = (f32[3,256,512]{2,1,0:T(8,128)}, f32[512,512]{1,0:T(8,128)}, f32[3,256,512]{2,1,0:T(8,128)}, f32[512,512]{1,0:T(8,128)}) async-done(((f32[3,256,512]{2,1,0:T(8,128)}, f32[512,512]{1,0:T(8,128)}, f32[3,256,512]{2,1,0:T(8,128)}, f32[512,512]{1,0:T(8,128)}), (f32[3,256,512]{2,1,0:T(8,128)}, f32[512,512]{1,0:T(8,128)}, f32[3,256,512]{2,1,0:T(8,128)}, ...) | async-done | bytes 5242896 | tf_op jit(solution)/shard_map/psum | solution.py:178
  678.2 114.3 %psum.77 = f32[]{:T(128)} all-reduce(f32[]{:T(128)} %select_reduce_fusion), channel_id=1, replica_groups=mesh['clip'=32,'tm'=8] {'clip'}, use_global_device_ids=true, to_apply=%region_5.6 | all-reduce | flops 1 | bytes 8 | tf_op jit(solution)/shard_map/psum | solution.py:178
  792.5 14.5 %psum.78 = f32[]{:T(128)} all-reduce(f32[]{:T(128)} %psum.77), channel_id=1, replica_groups=mesh['clip'=32,'tm'=8] {'tm'}, use_global_device_ids=true, to_apply=%region_6.7 | all-reduce | flops 1 | bytes 8 | tf_op jit(solution)/shard_map/psum | solution.py:177
  808.3 15.2 %all-reduce.10.cloned.1.call-done = (f32[3,256,512]{2,1,0:T(8,128)}, f32[512,512]{1,0:T(8,128)}, f32[3,256,512]{2,1,0:T(8,128)}, f32[512,512]{1,0:T(8,128)}) async-done(((f32[3,256,512]{2,1,0:T(8,128)}, f32[512,512]{1,0:T(8,128)}, f32[3,256,512]{2,1,0:T(8,128)}, f32[512,512]{1,0:T(8,128)}), (f32[3,256,512]{2,1,0:T(8,128)}, f32[512,512]{1,0:T(8,128)}, f32[3,256,512]{2,1,0:T(8,128)}, ...) | async-done | bytes 5242896 | tf_op jit(solution)/shard_map/psum | solution.py:177
  823.5 2.8 copy.1220
  (172 shorter events, 37.9 us)
Async XLA Ops:
  7.2 117.2 %copy-start = (bf16[3,256,512]{2,1,0:T(8,128)(2,1)S(1)}, bf16[3,256,512]{2,1,0:T(8,128)(2,1)}, u32[]{:S(2)}) copy-start(bf16[3,256,512]{2,1,0:T(8,128)(2,1)} %param.18) | copy-start | bytes 2359300
  7.2 669.6 %all-reduce.8.cloned.1.call-start = ((), (), s32[]{:S(2)}) async-start(), calls=%async_computation | async-start | bytes 10485760 | tf_op jit(solution)/shard_map/psum | solution.py:178
  8.1 114.0 %collective-permute-start = (bf16[2,4,1,256]{3,2,1,0:T(2,128)(2,1)S(1)}, bf16[2,4,1,256]{3,2,1,0:T(2,128)(2,1)S(1)}, u32[]{:S(2)}, u32[]{:S(2)}) collective-permute-start(bf16[2,4,1,256]{3,2,1,0:T(2,128)(2,1)S(1)} %get-tuple-element.49), channel_id=1, source_target_pairs={{0,1},{1,2},{2,3},{3,4},{4,5},{5,6},{6,7},{8,9},{9,10},{10,11},{11... | collective-permute-start | bytes 12296 | tf_op jit(solution)/shard_map/ppermute | solution.py:20
  9.8 112.3 %collective-permute-start.1 = (bf16[2,4,1,256]{3,2,1,0:T(2,128)(2,1)S(1)}, bf16[2,4,1,256]{3,2,1,0:T(2,128)(2,1)S(1)}, u32[]{:S(2)}, u32[]{:S(2)}) collective-permute-start(bf16[2,4,1,256]{3,2,1,0:T(2,128)(2,1)S(1)} %get-tuple-element.50), channel_id=1, source_target_pairs={{1,0},{2,1},{3,2},{4,3},{5,4},{6,5},{7,6},{9,8},{10,9},{11,10},{12... | collective-permute-start | bytes 12296 | tf_op jit(solution)/shard_map/ppermute | solution.py:22
  129.6 11.4 %copy-start.6 = (bf16[4,256,512]{2,1,0:T(8,128)(2,1)}, bf16[4,256,512]{2,1,0:T(8,128)(2,1)S(1)}, u32[]{:S(2)}) copy-start(bf16[4,256,512]{2,1,0:T(8,128)(2,1)S(1)} %convolution_convert_fusion) | copy-start | bytes 3145732
  129.6 8.2 collective-permute-start.2
  130.9 6.9 collective-permute-start.3
  135.1 5.9 copy-start.35
  137.8 5.2 copy-start.15
  137.8 5.1 copy-start.18
  149.3 3.1 copy-start.7
  149.3 3.1 copy-start.16
  149.3 3.1 copy-start.19
  161.4 4.6 copy-start.8
  161.4 4.6 copy-start.13
  161.4 4.6 copy-start.17
  161.4 4.6 copy-start.20
  165.9 10.3 %copy-start.4 = (bf16[768,1024]{1,0:T(8,128)(2,1)S(1)}, bf16[768,1024]{1,0:T(8,128)(2,1)}, u32[]{:S(2)}) copy-start(bf16[768,1024]{1,0:T(8,128)(2,1)} %copy.1171) | copy-start | bytes 4718596
  165.9 10.3 %copy-start.36 = (bf16[1024,512,1]{1,0,2:T(8,128)(2,1)S(1)}, bf16[1024,512,1]{1,0,2:T(8,128)(2,1)}, u32[]{:S(2)}) copy-start(bf16[1024,512,1]{1,0,2:T(8,128)(2,1)} %fusion.20) | copy-start | bytes 3145732
  168.1 11.8 %collective-permute-start.5 = (f32[4,15,512]{2,1,0:T(8,128)S(1)}, f32[4,15,512]{2,1,0:T(8,128)S(1)}, u32[]{:S(2)}, u32[]{:S(2)}) collective-permute-start(f32[4,15,512]{2,1,0:T(8,128)S(1)} %get-tuple-element.41), channel_id=1, source_target_pairs={{0,1},{1,2},{2,3},{3,4},{4,5},{5,6},{6,7},{8,9},{9,10},{10,11},{11... | collective-permute-start | bytes 368648 | tf_op jit(solution)/shard_map/ppermute | solution.py:32
  174.9 4.5 collective-permute-start.4
  187.2 636.3 %all-reduce.10.cloned.1.call-start = ((), (), s32[]{:S(2)}) async-start(), calls=%async_computation.1 | async-start | bytes 10485760 | tf_op jit(solution)/shard_map/psum | solution.py:177
  823.5 3.8 copy-start.5
  826.4 3.7 copy-start.1
  (25 other events, 42.2 us)
Sparse Core Ops, SparseCore 0:
  187.3 489.4 all-reduce.7
  679.7 143.7 all-reduce.9
